TPU v7x, 32 devices: a whole 2x2x4 slice. The times are simulated.
32 devices in a mesh: pipe: 8 (over z, y), head: 4 (over x, core).
Axes of the slice: x: 2, y: 2, z: 4, core: 2. Of those that a mesh axis runs over, the one named last changes fastest.
Arguments:
- queries: bfloat16 [2, 2048, 8192], P(None, 'pipe', 'head'), may hold values from -150 to 150
- keys: bfloat16 [2048, 1024], P(('pipe', 'head')), may hold values from -7 to 7
- values: bfloat16 [2048, 1024], P(('pipe', 'head')), may hold values from -6 to 6
- slice_index: int32 [2, 8], replicated, may hold values from 0 to 7, each once within a row
Outputs:
- attended: bfloat16 [2, 2048, 8192], P(None, 'pipe', 'head')
Inputs may be any that keep to these rules, and one draw needn't show every extreme that they name: Each row of slice_index is a permutation of 0 to 7.
All inputs are finite; a program needn't handle non-finite values.
Results may differ from a plain program's by a relative error of at most 0.0041.
Values may be sent and summed in bfloat16 or wider, within the bound.
A program may use at most 128 MiB of HBM per device.

v0:
```python
import math

import jax
import jax.numpy as jnp
from jax import lax
from jax.experimental import pallas as pl
from jax.experimental.pallas import tpu as pltpu
from jax.sharding import PartitionSpec as P

HEAD_SIZE = 128
NEG = -1e30
TO_EXP2 = HEAD_SIZE ** (-0.5) * math.log2(math.e)
PAIRS = 2
UNROLL = 4


def scores_of(query, key_block):
    return lax.dot_general(query, key_block, (((1,), (1,)), ((), ())), preferred_element_type=jnp.float32)


def weigh(scores, peak, value_block):
    weights = jnp.exp2((scores - peak) * TO_EXP2).astype(jnp.bfloat16)
    ones = jnp.ones(value_block.shape, jnp.bfloat16)
    return jnp.dot(weights, jnp.concatenate([value_block, ones], axis=1), preferred_element_type=jnp.float32)


MESH = pl.DeviceIdType.MESH


def fused_kernel(n_pipe, n_head, index_ref, q_ref, k_ref, v_ref, o_ref, kbuf, vbuf, qbuf, obuf, best_ref, accum_ref, local_sem, head_send, head_recv, left_send, right_send, side_send, chunk_recv, q_sem, out_sem):
    me = lax.axis_index("pipe")
    head = lax.axis_index("head")
    side = me + 1 - 2 * lax.rem(me, 2)
    row = lax.div(me, 2)
    line = n_pipe // 2
    has_left, has_right = row > 0, row < line - 1
    piece = k_ref.shape[0]
    rows = piece * n_head
    width = kbuf.shape[1]
    ins, bufs = (k_ref, v_ref), (kbuf, vbuf)

    barrier = pltpu.get_barrier_semaphore()
    for other in range(1, n_head):
        pl.semaphore_signal(barrier, inc=1, device_id=(me, lax.rem(head + other, n_head)), device_id_type=MESH)
    pl.semaphore_signal(barrier, inc=1, device_id=(side, head), device_id_type=MESH)

    @pl.when(has_left)
    def _():
        pl.semaphore_signal(barrier, inc=1, device_id=(me - 2, head), device_id_type=MESH)

    @pl.when(has_right)
    def _():
        pl.semaphore_signal(barrier, inc=1, device_id=(me + 2, head), device_id_type=MESH)

    pl.semaphore_wait(barrier, n_head + jnp.where(has_left, 1, 0) + jnp.where(has_right, 1, 0))

    def chunk(kind, owner):
        return bufs[kind].at[pl.ds(pl.multiple_of(owner * rows, rows), rows), :]

    def spot(kind, source):
        return bufs[kind].at[pl.ds(pl.multiple_of(me * rows + source * piece, piece), piece), :]

    def columns(kind, target):
        return ins[kind].at[:, pl.ds(pl.multiple_of(target * width, width), width)]

    def exchange(kind, other):
        return pltpu.make_async_remote_copy(
            columns(kind, lax.rem(head + other, n_head)), spot(kind, head),
            head_send.at[kind, other], head_recv.at[kind, other],
            device_id=(me, lax.rem(head + other, n_head)), device_id_type=MESH)

    def arrival(kind, other):
        source = lax.rem(head + n_head - other, n_head)
        return pltpu.make_async_remote_copy(
            columns(kind, head), spot(kind, source),
            head_send.at[kind, other], head_recv.at[kind, other],
            device_id=(me, source), device_id_type=MESH)

    def pass_on(kind, owner, target, sems):
        return pltpu.make_async_remote_copy(
            chunk(kind, owner), chunk(kind, owner), sems.at[kind, owner], chunk_recv.at[kind, owner],
            device_id=(target, head), device_id_type=MESH)

    def to_left(kind, owner):
        return pass_on(kind, owner, me - 2, left_send)

    def to_right(kind, owner):
        return pass_on(kind, owner, me + 2, right_send)

    def to_side(kind, owner):
        return pass_on(kind, owner, side, side_send)

    for kind in range(2):
        for other in range(1, n_head):
            exchange(kind, other).start()
        pltpu.make_async_copy(columns(kind, head), spot(kind, head), local_sem.at[kind]).start()
    pltpu.make_async_copy(q_ref, qbuf, q_sem).start()
    for kind in range(2):
        pltpu.make_async_copy(columns(kind, head), spot(kind, head), local_sem.at[kind]).wait()
        for other in range(1, n_head):
            arrival(kind, other).wait_recv()
        to_side(kind, me).start()

        @pl.when(has_left)
        def _():
            to_left(kind, me).start()

        @pl.when(has_right)
        def _():
            to_right(kind, me).start()

    def handle(step):
        for kind in range(2):

            @pl.when(row >= step)
            def _():
                owner = me - 2 * step
                to_right(kind, owner).wait_recv()
                to_side(kind, owner).start()

                @pl.when(has_right)
                def _():
                    to_right(kind, owner).start()

            @pl.when(row + step < line)
            def _():
                owner = me + 2 * step
                to_left(kind, owner).wait_recv()
                to_side(kind, owner).start()

                @pl.when(has_left)
                def _():
                    to_left(kind, owner).start()

    ticks, _, q_width = qbuf.shape
    heads = width // HEAD_SIZE
    group = q_width // width
    batches = group // UNROLL
    strip = UNROLL * HEAD_SIZE
    bodies = ticks * heads * batches
    pair_rows = 2 * rows
    steps = line // PAIRS
    diff = lax.broadcasted_iota(jnp.int32, (rows, pair_rows), 1) - lax.broadcasted_iota(jnp.int32, (rows, pair_rows), 0)
    reach = jnp.minimum(row, line - 1 - row)

    def nearest(place):
        offset = lax.div(place + 1, 2)
        near = jnp.where(lax.rem(place, 2) == 1, row - offset, row + offset)
        far = jnp.where(row < line - 1 - row, place, line - 1 - place)
        return jnp.where(place <= 2 * reach, near, far)

    def strip_out(item):
        tick = lax.div(item, heads * batches)
        at = pl.ds(pl.multiple_of(lax.rem(item, heads * batches) * strip, strip), strip)
        return pltpu.make_async_copy(obuf.at[tick, :, at], o_ref.at[tick, :, at], out_sem.at[item])

    def wide(array, count):
        return jnp.concatenate([array] * count, axis=1)

    def compute(step, first, last):
        pairs = [nearest(step * PAIRS + at) for at in range(PAIRS)]
        for pair in pairs:
            for kind in range(2):
                to_side(kind, 2 * pair + lax.rem(side, 2)).wait_recv()
        spans = [pl.ds(pl.multiple_of(pair * pair_rows, pair_rows), pair_rows) for pair in pairs]

        @pl.loop(0, bodies)
        def _(item):
            if not last:
                for at in range(PAIRS):
                    later = (step + 1) * PAIRS + at

                    @pl.when(item == (1 + 3 * at) * bodies // 8)
                    def _():
                        handle(later)

            tick = lax.div(item, heads * batches)
            strip_at = lax.rem(item, heads * batches)
            kv = pl.ds(pl.multiple_of(lax.div(strip_at, batches) * HEAD_SIZE, HEAD_SIZE), HEAD_SIZE)
            start = index_ref[tick, me] * rows
            for u in range(UNROLL):
                at = pl.ds(pl.multiple_of(strip_at * strip + u * HEAD_SIZE, HEAD_SIZE), HEAD_SIZE)
                slot = item * UNROLL + u
                query = qbuf[tick, :, at]
                scores = jnp.concatenate([
                    jnp.where(diff <= start - pair * pair_rows, scores_of(query, kbuf[span, kv]), NEG)
                    for pair, span in zip(pairs, spans)
                ], axis=1)
                top = jnp.broadcast_to(jnp.max(scores, axis=-1, keepdims=True), (rows, HEAD_SIZE))
                if first:
                    peak = top
                else:
                    before = best_ref[slot]
                    peak = jnp.maximum(before, top)
                block = jnp.concatenate([vbuf[span, kv] for span in spans], axis=0)
                result = weigh(scores, wide(peak, PAIRS * pair_rows // HEAD_SIZE), block)
                if not first:
                    result = result + accum_ref[slot] * wide(jnp.exp2((before - peak) * TO_EXP2), 2)
                if last:
                    obuf[tick, :, at] = (result[:, :HEAD_SIZE] / result[:, HEAD_SIZE:]).astype(obuf.dtype)
                else:
                    best_ref[slot] = peak
                    accum_ref[slot] = result
            if last:
                strip_out(item).start()

    handle(1)
    pltpu.make_async_copy(q_ref, qbuf, q_sem).wait()
    compute(0, True, steps == 1)
    if steps > 2:

        @pl.loop(1, steps - 1)
        def _(step):
            compute(step, False, False)

    if steps > 1:
        compute(steps - 1, False, True)

    for kind in range(2):
        for other in range(1, n_head):
            exchange(kind, other).wait_send()

    @pl.loop(0, line)
    def _(index):
        for kind in range(2):
            owner = 2 * index + lax.rem(me, 2)
            to_side(kind, owner).wait_send()

            @pl.when(jnp.logical_and(has_right, index <= row))
            def _():
                to_right(kind, owner).wait_send()

            @pl.when(jnp.logical_and(has_left, index >= row))
            def _():
                to_left(kind, owner).wait_send()

    @pl.loop(0, bodies)
    def _(item):
        strip_out(item).wait()


def on_device(sizes, queries, keys, values, slice_index):
    n_pipe, n_head = sizes
    ticks, rows, columns = queries.shape
    shape = (rows * n_pipe, keys.shape[1] // n_head)
    slots = ticks * columns // HEAD_SIZE
    whole = pl.BlockSpec(memory_space=pltpu.VMEM)
    anywhere = pl.BlockSpec(memory_space=pl.ANY)
    dma = pltpu.SemaphoreType.DMA
    return pl.pallas_call(
        lambda *refs: fused_kernel(n_pipe, n_head, *refs),
        out_shape=jax.ShapeDtypeStruct(queries.shape, queries.dtype),
        in_specs=[pl.BlockSpec(memory_space=pltpu.SMEM), anywhere, whole, whole],
        out_specs=anywhere,
        scratch_shapes=[
            pltpu.VMEM(shape, keys.dtype),
            pltpu.VMEM(shape, keys.dtype),
            pltpu.VMEM(queries.shape, queries.dtype),
            pltpu.VMEM(queries.shape, queries.dtype),
            pltpu.VMEM((slots, rows, HEAD_SIZE), jnp.float32),
            pltpu.VMEM((slots, rows, 2 * HEAD_SIZE), jnp.float32),
            dma((2,)),
            dma((2, n_head)),
            dma((2, n_head)),
            dma((2, n_pipe)),
            dma((2, n_pipe)),
            dma((2, n_pipe)),
            dma((2, n_pipe)),
            dma,
            dma((slots // UNROLL,)),
        ],
        compiler_params=pltpu.CompilerParams(collective_id=0, has_side_effects=True, vmem_limit_bytes=60 * 2 ** 20),
        name="fused",
    )(slice_index, queries, keys, values)


def solution(mesh):
    sizes = (mesh.shape["pipe"], mesh.shape["head"])
    return jax.shard_map(
        lambda *arrays: on_device(sizes, *arrays),
        mesh=mesh,
        in_specs=(
            P(None, "pipe", "head"),
            P(("pipe", "head"), None),
            P(("pipe", "head"), None),
            P(),
        ),
        out_specs=P(None, "pipe", "head"),
        check_vma=False,
    )
```

profile of v0, /device:TPU:0, one launch (start us, length us, event | category | flops | bytes accessed | tf_op | source)
XLA Modules:
  0.0 61.6 jit_solution(13817114575422769423)
XLA Ops:
  0.0 58.4 %fused.1 = bf16[2,256,2048]{2,1,0:T(8,128)(2,1)} custom-call(s32[2,8]{1,0:T(2,128)} %refs_0_.1, bf16[2,256,2048]{2,1,0:T(8,128)(2,1)} %refs_1_.1, bf16[64,1024]{1,0:T(8,128)(2,1)} %refs_2_.1, bf16[64,1024]{1,0:T(8,128)(2,1)} %refs_3_.1), custom_call_target="tpu_custom_call" | custom-call | tf_op jit(solution)/shard_map/fused/pallas_call | solution.py:250
  58.4 3.2 %copy.6 = bf16[2,256,2048]{2,1,0:T(8,128)(2,1)} copy(bf16[2,256,2048]{2,1,0:T(8,128)(2,1)} %fused.1) | data formatting | bytes 4194304
where the time goes:
time: 61.7 us; the launch traced here: 61.6 us
  Pallas kernels  58.4 us (95%)
  local copies, waits for them, and re-layouts  3.16 us (5%)
    pallas_call x1, Pallas kernels, on_device(): pl.pallas_call(lambda *refs: fused_kernel(n_pipe, n_head, *refs), out_sha...  58.4 us
    unnamed x1, local copies, waits for them, and re-layouts  3.16 us

commit v1 on v0

--- a/solution.py
+++ b/solution.py
@@ -11,7 +11,7 @@
 NEG = -1e30
 TO_EXP2 = HEAD_SIZE ** (-0.5) * math.log2(math.e)
 PAIRS = 2
-UNROLL = 4
+UNROLL = 8
 
 
 def scores_of(query, key_block):

time: 61.7 us -> 56.5 us (0.916)
  Pallas kernels: 58.4 us -> 53.2 us
    pallas_call x1, Pallas kernels: 58.4 us -> 53.2 us  [on_device(): pl.pallas_call(lambda *refs: fused_kernel(n_pipe, n_head, *refs), out_sha...]
where the time goes in v1:
time: 56.5 us; the launch traced here: 56.4 us
  Pallas kernels  53.2 us (94%)
  local copies, waits for them, and re-layouts  3.16 us (6%)
    pallas_call x1, Pallas kernels, on_device(): pl.pallas_call(lambda *refs: fused_kernel(n_pipe, n_head, *refs), out_sha...  53.2 us
    unnamed x1, local copies, waits for them, and re-layouts  3.16 us

profile of v1, /device:TPU:0, one launch (start us, length us, event | category | flops | bytes accessed | tf_op | source)
XLA Modules:
  0.0 56.4 jit_solution(2124371044938052432)
XLA Ops:
  0.0 53.2 %fused.1 = bf16[2,256,2048]{2,1,0:T(8,128)(2,1)} custom-call(s32[2,8]{1,0:T(2,128)} %refs_0_.1, bf16[2,256,2048]{2,1,0:T(8,128)(2,1)} %refs_1_.1, bf16[64,1024]{1,0:T(8,128)(2,1)} %refs_2_.1, bf16[64,1024]{1,0:T(8,128)(2,1)} %refs_3_.1), custom_call_target="tpu_custom_call" | custom-call | tf_op jit(solution)/shard_map/fused/pallas_call | solution.py:250
  53.2 3.2 %copy.6 = bf16[2,256,2048]{2,1,0:T(8,128)(2,1)} copy(bf16[2,256,2048]{2,1,0:T(8,128)(2,1)} %fused.1) | data formatting | bytes 4194304
